TPU v7x, 32 devices: a whole 2x2x4 slice. The times are simulated.
32 devices in a mesh: shots: 2 (over y), wide: 16 (over z, x, core).
Axes of the slice: x: 2, y: 2, z: 4, core: 2. Of those that a mesh axis runs over, the one named last changes fastest.
Arguments:
- src_now: float32 [32, 64, 128], P('wide', 'shots'), parts along dimension 1, may hold values from -6 to 6
- src_old: float32 [32, 64, 128], P('wide', 'shots'), parts along dimension 1, may hold values from -6 to 6
- rcv_now: float32 [32, 256, 32], P('wide', 'shots'), parts along dimension 1, may hold values from -6 to 6
- rcv_old: float32 [32, 256, 32], P('wide', 'shots'), parts along dimension 1, may hold values from -6 to 6
- medium: float32 [3, 32, 128, 32], P(None, 'wide'), may hold values from 0.04 to 0.24
- wavelet: float32 [4], replicated, may hold values from -4 to 4
- shot: int32 [6], P('shots'), parts along dimension 0, may hold values from 0 to 31
- traces: float32 [32, 128, 4], P('wide', 'shots'), parts along dimension 1, may hold values from -6 to 6
- rec_x: int32 [32, 128], P('wide', 'shots'), parts along dimension 1, may hold values from 0 to 31
- lag_order: int32 [33], replicated, may hold values from 0 to 32, each once
Outputs:
- src_next: float32 [32, 64, 128], P('wide', 'shots'), parts along dimension 1
- src_prior: float32 [32, 64, 128], P('wide', 'shots'), parts along dimension 1
- rcv_next: float32 [32, 256, 32], P('wide', 'shots'), parts along dimension 1
- rcv_prior: float32 [32, 256, 32], P('wide', 'shots'), parts along dimension 1
- image: float32 [66, 32, 128, 32], P('shots', 'wide'), parts along dimension 0
There are 2 independent parts, one for each index of `shots`. A program takes and returns all parts, laid end to end along the dimension named above; an argument that names none is the same for every part. Nothing has to cross between parts.
Inputs may be any that keep to these rules, and one draw needn't show every extreme that they name: `lag_order`: each of the 33 lag slots once.
All inputs are finite; a program needn't handle non-finite values.
Results may differ from a plain program's by a relative error of at most 0.0003.
Values sent between devices are 32-bit elements; how exact they have to be, the bound alone decides.
A program may use at most 64 MiB of HBM per device.

v0:
```python
import jax
import jax.numpy as jnp
from jax import lax
from jax.sharding import PartitionSpec as P


def extended(array, sides, width):
    for axis, dim in sides:
        devices, length = (lax.axis_size(axis), array.shape[dim])
        up = [(i, (i + 1) % devices) for i in range(devices - 1)]
        down = [(j, i) for i, j in up]
        last = lax.slice_in_dim(array, length - width, length, axis=dim)
        initial = lax.slice_in_dim(array, 0, width, axis=dim)
        before = lax.ppermute(last, axis, up)
        after = lax.ppermute(initial, axis, down)
        array = jnp.concatenate([before, array, after], axis=dim)
    return array


def window_sum(padded, dim, count):

    def window_at(start):
        return lax.slice_in_dim(padded, start, start + count, axis=dim)

    return (
        -1.0 / 12.0 * (window_at(0) + window_at(4))
        + 4.0 / 3.0 * (window_at(1) + window_at(3))
        - 2.5 * window_at(2)
    )


def widen(field, dim):
    widths = [(0, 0)] * field.ndim
    widths[dim] = (2, 2)
    return jnp.pad(field, widths)


def second(field, dim):
    return window_sum(widen(field, dim), dim, field.shape[dim])


def lagged(snaps, lag_order):
    half = (lag_order.shape[0] - 1) // 2
    cells_x = snaps[0][0].shape[2]
    widths = ((0, 0), (0, 0), (half, half))
    padded = [(jnp.pad(source, widths), jnp.pad(receiver, widths)) for source, receiver in snaps]

    def one_plane(slot):
        offset = slot - half
        total = None
        for source, receiver in padded:
            moved_src = lax.dynamic_slice_in_dim(source, half - offset, cells_x, 2)
            moved_rcv = lax.dynamic_slice_in_dim(receiver, half + offset, cells_x, 2)
            product = moved_src * moved_rcv
            total = product if total is None else total + product
        return total

    return lax.map(one_plane, lag_order)


def indicator(count, first, target):
    return (jnp.arange(count, dtype=jnp.int32) + first == target).astype(jnp.float32)


def on_device(src_now, src_old, rcv_now, rcv_old, medium, wavelet, shot, traces, rec_x, lag_order):
    slab_x, cells_y, cells_z = src_now.shape
    slab_y, _, cells_x = rcv_now.shape
    device = lax.axis_index("wide")
    steps = wavelet.shape[0]
    onehot = (rec_x[:, :, None] == jnp.arange(cells_x, dtype=jnp.int32)[None, None, :]).astype(
        jnp.float32
    )
    shot_rcv = (
        indicator(slab_y, device * slab_y, shot[1])[:, None, None]
        * indicator(cells_z, 0, shot[2])[None, :, None]
        * indicator(cells_x, 0, shot[0])[None, None, :]
    )
    snaps = []
    turned_now, turned_old = (
        lax.all_to_all(src_now, "wide", split_axis=1, concat_axis=0, tiled=True),
        lax.all_to_all(src_old, "wide", split_axis=1, concat_axis=0, tiled=True),
    )
    pair_now = jnp.stack([jnp.transpose(turned_now, (1, 2, 0)), rcv_now])
    pair_old = jnp.stack([jnp.transpose(turned_old, (1, 2, 0)), rcv_old])
    for step in range(steps):
        widened = extended(pair_now, (("wide", 1),), 2)
        spread = (
            medium[0] * second(pair_now, 3)
            + medium[1] * window_sum(widened, 1, slab_y)
            + medium[2] * second(pair_now, 2)
        )
        pair_new = 2.0 * pair_now - pair_old + spread
        pair_new = pair_new.at[0].add(-wavelet[step] * shot_rcv)
        pair_new = pair_new.at[1, :, 0, :].add(
            jnp.einsum("yr,yrx->yx", traces[:, :, step], onehot, precision=lax.Precision.HIGHEST)
        )
        pair_old, pair_now = (pair_now, pair_new)
        if step % 2 == 1:
            snaps.append((pair_now[0], pair_now[1]))
    back_now, back_old = (
        lax.all_to_all(pair_now[0], "wide", split_axis=2, concat_axis=0, tiled=True),
        lax.all_to_all(pair_old[0], "wide", split_axis=2, concat_axis=0, tiled=True),
    )
    src_next = jnp.transpose(back_now, (2, 0, 1))
    src_prior = jnp.transpose(back_old, (2, 0, 1))
    return (src_next, src_prior, pair_now[1], pair_old[1], lagged(snaps, lag_order))


def solution(mesh):
    return jax.shard_map(
        on_device,
        mesh=mesh,
        in_specs=(
            P("wide", "shots", None),
            P("wide", "shots", None),
            P("wide", "shots", None),
            P("wide", "shots", None),
            P(None, "wide", None, None),
            P(),
            P("shots"),
            P("wide", "shots", None),
            P("wide", "shots"),
            P(),
        ),
        out_specs=(
            P("wide", "shots", None),
            P("wide", "shots", None),
            P("wide", "shots", None),
            P("wide", "shots", None),
            P("shots", "wide", None, None),
        ),
        check_vma=False,
    )
```

profile of v0, /device:TPU:0, one launch (start us, length us, event | category | flops | bytes accessed | tf_op | source)
XLA Modules:
  0.0 220.2 jit_solution(10086139652803222354)
XLA Ops:
  0.7 1.4 copy.55
  2.1 7.4 %all-to-all-start = ((f32[2,32,128]{2,0,1:T(2,128)}), f32[2,32,128]{2,0,1:T(2,128)S(1)}, u32[]{:S(2)}, u32[]{:S(2)}) async-start(f32[2,32,128]{2,0,1:T(2,128)} %copy.55), calls=%async_computation | async-start | bytes 65536 | tf_op jit(solution)/shard_map/all_to_all | solution.py:80
  9.5 0.8 slice_bitcast_fusion.8
  10.3 1.4 copy.57
  11.7 1.4 fusion.109
  13.0 0.6 compare_convert_fusion.1
  13.7 0.7 compare_convert_fusion.2
  14.4 1.4 fusion.108
  16.5 6.0 %all-to-all-start.1 = ((f32[2,32,128]{2,0,1:T(2,128)}), f32[2,32,128]{2,0,1:T(2,128)S(1)}, u32[]{:S(2)}, u32[]{:S(2)}) async-start(f32[2,32,128]{2,0,1:T(2,128)} %copy.57), calls=%async_computation.1 | async-start | bytes 65536 | tf_op jit(solution)/shard_map/all_to_all | solution.py:81
  22.5 0.8 pad_maximum_fusion.10
  23.3 2.3 %collective-permute-start = (f32[2,2,128,32]{2,3,1,0:T(8,128)S(1)}, f32[2,2,128,32]{2,3,1,0:T(8,128)S(1)}, u32[]{:S(2)}, u32[]{:S(2)}) collective-permute-start(f32[2,2,128,32]{2,3,1,0:T(8,128)S(1)} %pad_maximum_fusion.10), channel_id=1, source_target_pairs={{0,1},{1,2},{2,3},{3,4},{4,5},{5,6},{6,7},{7,8},{8,9},{9,10},{10,1... | collective-permute-start | bytes 196616 | tf_op jit(solution)/shard_map/ppermute | solution.py:14
  25.6 1.3 collective-permute-start.1
  26.9 0.7 compare_convert_fusion
  27.5 1.6 all-to-all-done.1
  29.1 0.7 collective-permute-done.1
  29.9 0.9 fusion.11
  31.3 4.8 %collective-permute-start.2 = (f32[2,2,128,32]{2,3,1,0:T(8,128)S(1)}, f32[2,2,128,32]{2,3,1,0:T(8,128)S(1)}, u32[]{:S(2)}, u32[]{:S(2)}) collective-permute-start(f32[2,2,128,32]{2,3,1,0:T(8,128)S(1)} %scatter-add.29), channel_id=1, source_target_pairs={{0,1},{1,2},{2,3},{3,4},{4,5},{5,6},{6,7},{7,8},{8,9},{9,10},{10,1... | collective-permute-start | bytes 196616 | tf_op jit(solution)/shard_map/ppermute | solution.py:14
  36.2 1.3 collective-permute-start.3
  38.1 1.2 collective-permute-done.3
  40.0 5.1 %collective-permute-start.4 = (f32[2,2,128,32]{2,3,1,0:T(8,128)S(1)}, f32[2,2,128,32]{2,3,1,0:T(8,128)S(1)}, u32[]{:S(2)}, u32[]{:S(2)}) collective-permute-start(f32[2,2,128,32]{2,3,1,0:T(8,128)S(1)} %scatter-add.31), channel_id=1, source_target_pairs={{0,1},{1,2},{2,3},{3,4},{4,5},{5,6},{6,7},{7,8},{8,9},{9,10},{10,1... | collective-permute-start | bytes 196616 | tf_op jit(solution)/shard_map/ppermute | solution.py:14
  45.1 1.3 collective-permute-start.5
  48.9 5.3 %collective-permute-start.6 = (f32[2,2,128,32]{2,3,1,0:T(8,128)S(1)}, f32[2,2,128,32]{2,3,1,0:T(8,128)S(1)}, u32[]{:S(2)}, u32[]{:S(2)}) collective-permute-start(f32[2,2,128,32]{2,3,1,0:T(8,128)S(1)} %scatter-add.35), channel_id=1, source_target_pairs={{0,1},{1,2},{2,3},{3,4},{4,5},{5,6},{6,7},{7,8},{8,9},{9,10},{10,1... | collective-permute-start | bytes 196616 | tf_op jit(solution)/shard_map/ppermute | solution.py:14
  54.1 1.3 collective-permute-start.7
  56.1 0.6 copy.66
  56.7 7.4 %all-to-all-start.3 = ((f32[2,128,32]{1,0,2:T(2,128)}), f32[2,128,32]{1,0,2:T(2,128)S(1)}, u32[]{:S(2)}, u32[]{:S(2)}) async-start(f32[2,128,32]{1,0,2:T(2,128)} %copy.66), calls=%async_computation.3 | async-start | bytes 65536 | tf_op jit(solution)/shard_map/all_to_all | solution.py:102
  64.2 6.6 %all-to-all-done.3 = f32[2,128,32]{1,0,2:T(2,128)S(1)} async-done(((f32[2,128,32]{1,0,2:T(2,128)}), f32[2,128,32]{1,0,2:T(2,128)S(1)}, u32[]{:S(2)}, u32[]{:S(2)}) %all-to-all-start.3) | async-done | bytes 32800 | tf_op jit(solution)/shard_map/all_to_all | solution.py:102
  70.8 0.6 copy.68
  72.1 0.6 copy.63
  72.8 3.5 %all-to-all-start.2 = ((f32[2,128,32]{1,0,2:T(2,128)}), f32[2,128,32]{1,0,2:T(2,128)S(1)}, u32[]{:S(2)}, u32[]{:S(2)}) async-start(f32[2,128,32]{1,0,2:T(2,128)} %copy.63), calls=%async_computation.2 | async-start | bytes 65536 | tf_op jit(solution)/shard_map/all_to_all | solution.py:101
  76.3 143.2 %while.23 = (s32[]{:T(128)}, f32[33,2,128,32]{2,3,1,0:T(8,128)}, s32[33]{0:T(128)S(1)}, f32[2,128,64]{1,2,0:T(8,128)S(1)}, f32[2,128,64]{1,2,0:T(8,128)S(1)}, /*...) while((s32[]{:T(128)}, f32[33,2,128,32]{2,3,1,0:T(8,128)}, ...), condition=%wide.region_1.2_spmd, body=%wide.region_0.1_spmd.sunk | while | flops 24586 | bytes 819957 | solution.py:58
  80.0 0.6 constant_dynamic-update-slice_fusion.2
  84.3 0.6 constant_dynamic-update-slice_fusion.2
  88.7 0.6 constant_dynamic-update-slice_fusion.2
  93.0 0.6 constant_dynamic-update-slice_fusion.2
  97.4 0.6 constant_dynamic-update-slice_fusion.2
  101.7 0.6 constant_dynamic-update-slice_fusion.2
  106.0 0.6 constant_dynamic-update-slice_fusion.2
  114.7 0.6 constant_dynamic-update-slice_fusion.2
  119.1 0.6 constant_dynamic-update-slice_fusion.2
  127.7 0.6 constant_dynamic-update-slice_fusion.2
  132.1 0.6 constant_dynamic-update-slice_fusion.2
  136.4 0.6 constant_dynamic-update-slice_fusion.2
  140.8 0.6 constant_dynamic-update-slice_fusion.2
  145.1 0.6 constant_dynamic-update-slice_fusion.2
  149.4 0.6 constant_dynamic-update-slice_fusion.2
  153.8 0.6 constant_dynamic-update-slice_fusion.2
  158.1 0.6 constant_dynamic-update-slice_fusion.2
  219.5 0.6 copy.65
  (359 shorter events, 51.2 us)
Async XLA Ops:
  0.6 38.7 %copy-start = (f32[2,128,32]{1,2,0:T(8,128)S(1)}, f32[2,128,32]{1,2,0:T(8,128)}, u32[]{:S(2)}) copy-start(f32[2,128,32]{1,2,0:T(8,128)} %param.30) | copy-start | bytes 98308
  0.6 30.2 %copy-start.2 = (f32[2,64,4]{1,2,0:T(4,128)S(1)}, f32[2,64,4]{1,2,0:T(4,128)}, u32[]{:S(2)}) copy-start(f32[2,64,4]{1,2,0:T(4,128)} %param.35) | copy-start | bytes 6148
  0.7 30.2 %copy-start.3 = (s32[2,64]{1,0:T(2,128)S(1)}, s32[2,64]{1,0:T(2,128)}, u32[]{:S(2)}) copy-start(s32[2,64]{1,0:T(2,128)} %param.36) | copy-start | bytes 1540
  2.1 14.4 %all-to-all-start = ((f32[2,32,128]{2,0,1:T(2,128)}), f32[2,32,128]{2,0,1:T(2,128)S(1)}, u32[]{:S(2)}, u32[]{:S(2)}) async-start(f32[2,32,128]{2,0,1:T(2,128)} %copy.55), calls=%async_computation | async-start | bytes 65536 | tf_op jit(solution)/shard_map/all_to_all | solution.py:80
  16.5 12.7 %all-to-all-start.1 = ((f32[2,32,128]{2,0,1:T(2,128)}), f32[2,32,128]{2,0,1:T(2,128)S(1)}, u32[]{:S(2)}, u32[]{:S(2)}) async-start(f32[2,32,128]{2,0,1:T(2,128)} %copy.57), calls=%async_computation.1 | async-start | bytes 65536 | tf_op jit(solution)/shard_map/all_to_all | solution.py:81
  23.3 5.9 %collective-permute-start = (f32[2,2,128,32]{2,3,1,0:T(8,128)S(1)}, f32[2,2,128,32]{2,3,1,0:T(8,128)S(1)}, u32[]{:S(2)}, u32[]{:S(2)}) collective-permute-start(f32[2,2,128,32]{2,3,1,0:T(8,128)S(1)} %pad_maximum_fusion.10), channel_id=1, source_target_pairs={{0,1},{1,2},{2,3},{3,4},{4,5},{5,6},{6,7},{7,8},{8,9},{9,10},{10,1... | collective-permute-start | bytes 196616 | tf_op jit(solution)/shard_map/ppermute | solution.py:14
  25.6 4.3 %collective-permute-start.1 = (f32[2,2,128,32]{2,3,1,0:T(8,128)S(1)}, f32[2,2,128,32]{2,3,1,0:T(8,128)S(1)}, u32[]{:S(2)}, u32[]{:S(2)}) collective-permute-start(f32[2,2,128,32]{2,3,1,0:T(8,128)S(1)} %pad_maximum_fusion.10), channel_id=1, source_target_pairs={{1,0},{2,1},{3,2},{4,3},{5,4},{6,5},{7,6},{8,7},{9,8},{10,9},{11,1... | collective-permute-start | bytes 196616 | tf_op jit(solution)/shard_map/ppermute | solution.py:15
  31.3 6.8 %collective-permute-start.2 = (f32[2,2,128,32]{2,3,1,0:T(8,128)S(1)}, f32[2,2,128,32]{2,3,1,0:T(8,128)S(1)}, u32[]{:S(2)}, u32[]{:S(2)}) collective-permute-start(f32[2,2,128,32]{2,3,1,0:T(8,128)S(1)} %scatter-add.29), channel_id=1, source_target_pairs={{0,1},{1,2},{2,3},{3,4},{4,5},{5,6},{6,7},{7,8},{8,9},{9,10},{10,1... | collective-permute-start | bytes 196616 | tf_op jit(solution)/shard_map/ppermute | solution.py:14
  36.2 3.1 %collective-permute-start.3 = (f32[2,2,128,32]{2,3,1,0:T(8,128)S(1)}, f32[2,2,128,32]{2,3,1,0:T(8,128)S(1)}, u32[]{:S(2)}, u32[]{:S(2)}) collective-permute-start(f32[2,2,128,32]{2,3,1,0:T(8,128)S(1)} %scatter-add.29), channel_id=1, source_target_pairs={{1,0},{2,1},{3,2},{4,3},{5,4},{6,5},{7,6},{8,7},{9,8},{10,9},{11,1... | collective-permute-start | bytes 196616 | tf_op jit(solution)/shard_map/ppermute | solution.py:15
  40.0 7.7 %collective-permute-start.4 = (f32[2,2,128,32]{2,3,1,0:T(8,128)S(1)}, f32[2,2,128,32]{2,3,1,0:T(8,128)S(1)}, u32[]{:S(2)}, u32[]{:S(2)}) collective-permute-start(f32[2,2,128,32]{2,3,1,0:T(8,128)S(1)} %scatter-add.31), channel_id=1, source_target_pairs={{0,1},{1,2},{2,3},{3,4},{4,5},{5,6},{6,7},{7,8},{8,9},{9,10},{10,1... | collective-permute-start | bytes 196616 | tf_op jit(solution)/shard_map/ppermute | solution.py:14
  45.1 3.1 %collective-permute-start.5 = (f32[2,2,128,32]{2,3,1,0:T(8,128)S(1)}, f32[2,2,128,32]{2,3,1,0:T(8,128)S(1)}, u32[]{:S(2)}, u32[]{:S(2)}) collective-permute-start(f32[2,2,128,32]{2,3,1,0:T(8,128)S(1)} %scatter-add.31), channel_id=1, source_target_pairs={{1,0},{2,1},{3,2},{4,3},{5,4},{6,5},{7,6},{8,7},{9,8},{10,9},{11,1... | collective-permute-start | bytes 196616 | tf_op jit(solution)/shard_map/ppermute | solution.py:15
  48.4 27.9 %copy-start.4 = (s32[33]{0:T(128)S(1)}, s32[33]{0:T(128)}, u32[]{:S(2)}) copy-start(s32[33]{0:T(128)} %param.37) | copy-start | bytes 400
  48.9 22.5 %collective-permute-start.6 = (f32[2,2,128,32]{2,3,1,0:T(8,128)S(1)}, f32[2,2,128,32]{2,3,1,0:T(8,128)S(1)}, u32[]{:S(2)}, u32[]{:S(2)}) collective-permute-start(f32[2,2,128,32]{2,3,1,0:T(8,128)S(1)} %scatter-add.35), channel_id=1, source_target_pairs={{0,1},{1,2},{2,3},{3,4},{4,5},{5,6},{6,7},{7,8},{8,9},{9,10},{10,1... | collective-permute-start | bytes 196616 | tf_op jit(solution)/shard_map/ppermute | solution.py:14
  54.1 17.3 %collective-permute-start.7 = (f32[2,2,128,32]{2,3,1,0:T(8,128)S(1)}, f32[2,2,128,32]{2,3,1,0:T(8,128)S(1)}, u32[]{:S(2)}, u32[]{:S(2)}) collective-permute-start(f32[2,2,128,32]{2,3,1,0:T(8,128)S(1)} %scatter-add.35), channel_id=1, source_target_pairs={{1,0},{2,1},{3,2},{4,3},{5,4},{6,5},{7,6},{8,7},{9,8},{10,9},{11,1... | collective-permute-start | bytes 196616 | tf_op jit(solution)/shard_map/ppermute | solution.py:15
  56.7 14.0 %all-to-all-start.3 = ((f32[2,128,32]{1,0,2:T(2,128)}), f32[2,128,32]{1,0,2:T(2,128)S(1)}, u32[]{:S(2)}, u32[]{:S(2)}) async-start(f32[2,128,32]{1,0,2:T(2,128)} %copy.66), calls=%async_computation.3 | async-start | bytes 65536 | tf_op jit(solution)/shard_map/all_to_all | solution.py:102
  72.1 4.2 %copy-start.1 = (f32[2,128,32]{1,2,0:T(8,128)}, f32[2,128,32]{1,2,0:T(8,128)S(1)}, u32[]{:S(2)}) copy-start(f32[2,128,32]{1,2,0:T(8,128)S(1)} %get-tuple-element.340) | copy-start | bytes 98308
  72.8 146.7 %all-to-all-start.2 = ((f32[2,128,32]{1,0,2:T(2,128)}), f32[2,128,32]{1,0,2:T(2,128)S(1)}, u32[]{:S(2)}, u32[]{:S(2)}) async-start(f32[2,128,32]{1,0,2:T(2,128)} %copy.63), calls=%async_computation.2 | async-start | bytes 65536 | tf_op jit(solution)/shard_map/all_to_all | solution.py:101
where the time goes:
time: 224 us; the launch traced here: 220 us
  loops' own time  85 us (38%)
  local copies, waits for them, and re-layouts  67.3 us (30%)
  starting transfers between devices  47 us (21%)
  waiting for transfers between devices  10.6 us (5%)
  other arithmetic  5.48 us (2%)
  between operations  3.54 us (2%)
    another operation x1, loops' own time, lagged(): return lax.map(one_plane, lag_order)  85 us
    dynamic_update_slice x66, local copies, waits for them, and re-layouts, lagged(): return lax.map(one_plane, lag_order)  23 us
    dynamic_slice x33, local copies, waits for them, and re-layouts, lagged(): return lax.map(one_plane, lag_order)  19.9 us
    ppermute x4, starting transfers between devices, extended(): before = lax.ppermute(last, axis, up)  17.5 us
    dynamic_slice x132, local copies, waits for them, and re-layouts, one_plane(): moved_rcv = lax.dynamic_slice_in_dim(receiver, half + offset, cells_x, 2)  7.68 us
    all_to_all x1, starting transfers between devices, on_device(): lax.all_to_all(pair_old[0], 'wide', split_axis=2, concat_axis=0, tiled=True)  7.41 us
    all_to_all x1, starting transfers between devices, on_device(): lax.all_to_all(src_now, 'wide', split_axis=1, concat_axis=0, tiled=True)  7.39 us
    all_to_all x1, waiting for transfers between devices, on_device(): lax.all_to_all(pair_old[0], 'wide', split_axis=2, concat_axis=0, tiled=True)  6.59 us
  transfers between devices with their start and end apart: 12, of which 5 were waited for; matrix products, arithmetic and copies ran while one was open for 31% of the time, Pallas kernels for 0%

commit v1 on v0

v1 whole, which is shorter than its diff:
```python
import functools

import jax
import jax.numpy as jnp
from jax import lax
from jax.experimental import pallas as pl
from jax.experimental.pallas import tpu as pltpu
from jax.sharding import PartitionSpec as P

REACH = 2
EDGE = 8
OUTER, INNER, CENTRE = -1.0 / 12.0, 4.0 / 3.0, -2.5
SRC, RCV = 0, 1


def second(window):
    return (
        OUTER * (window(-2) + window(2)) + INNER * (window(-1) + window(1)) + CENTRE * window(0)
    )


def window_kernel(
    devices,
    src_now,
    src_old,
    rcv_now,
    rcv_old,
    medium,
    wavelet,
    shot,
    traces,
    rec_x,
    src_next,
    src_prior,
    rcv_next,
    rcv_prior,
    snaps,
    staged,
    landed,
    levels,
    partial,
    surface,
    spot,
    leaving,
    returned,
    out_send,
    out_recv,
    back_send,
    back_recv,
    halo_send,
    halo_recv,
):
    me = lax.axis_index("wide")
    slab_x, cells_y, cells_z = src_now.shape
    slab_y, cells_x, _ = rcv_now.shape
    steps = wavelet.shape[0]
    span = slab_y + 2 * REACH
    rows = staged.shape[0] // (devices * slab_x)
    block = slab_x * rows
    back_rows = 2 * slab_x * slab_y
    inside = pl.ds(EDGE, cells_x)

    barrier = pltpu.get_barrier_semaphore()

    @pl.loop(1, devices)
    def _(distance):
        pl.semaphore_signal(
            barrier,
            inc=1,
            device_id={"wide": lax.rem(me + distance, devices)},
            device_id_type=MESH,
        )

    for peer in range(devices):
        first = peer * slab_y - REACH
        low, high = max(first, 0), min(first + span, cells_y)
        for x in range(slab_x):
            base = (peer * slab_x + x) * rows
            if low > first or high < first + span:
                staged[base : base + rows, :] = jnp.zeros((rows, cells_z), jnp.float32)
            staged[base + low - first : base + high - first, :] = src_now[x, low:high, :]
            staged[base + span : base + span + slab_y, :] = src_old[
                x, peer * slab_y : (peer + 1) * slab_y, :
            ]

    zero_edge = jnp.zeros((EDGE, cells_z), jnp.float32)
    zero_plane = jnp.zeros((cells_x, cells_z), jnp.float32)
    for level in range(steps):
        for field in (SRC, RCV):
            for y in range(REACH, REACH + slab_y):
                levels[level, field, y, 0:EDGE, :] = zero_edge
                levels[level, field, y, EDGE + cells_x : EDGE + cells_x + EDGE, :] = zero_edge

    @pl.when(me == 0)
    def _():
        for level in range(steps):
            for field in (SRC, RCV):
                for y in range(REACH):
                    levels[level, field, y, inside, :] = zero_plane

    @pl.when(me == devices - 1)
    def _():
        for level in range(steps):
            for field in (SRC, RCV):
                for y in range(REACH):
                    levels[level, field, REACH + slab_y + y, inside, :] = zero_plane

    for y in range(slab_y):
        levels[0, RCV, REACH + y, inside, :] = rcv_now[y]

    pl.semaphore_wait(barrier, devices - 1)

    def out_copy(peer):
        return pltpu.make_async_remote_copy(
            src_ref=staged.at[pl.ds(pl.multiple_of(peer * block, 8), block)],
            dst_ref=landed.at[pl.ds(pl.multiple_of(me * block, 8), block)],
            send_sem=out_send,
            recv_sem=out_recv,
            device_id={"wide": peer},
            device_id_type=MESH,
        )

    def halo_copy(field, level, side):
        if level == 0:
            first = slab_y - REACH if side == 0 else 0
            source = rcv_now.at[pl.ds(first, REACH)]
        else:
            first = slab_y if side == 0 else REACH
            source = levels.at[level, field, pl.ds(first, REACH), inside]
        into = 0 if side == 0 else REACH + slab_y
        peer = me + 1 if side == 0 else me - 1
        return pltpu.make_async_remote_copy(
            src_ref=source,
            dst_ref=levels.at[level, field, pl.ds(into, REACH), inside],
            send_sem=halo_send.at[field, level, side],
            recv_sem=halo_recv.at[field, level, side],
            device_id={"wide": peer},
            device_id_type=MESH,
        )

    def each_side(field, level, act):
        @pl.when(me < devices - 1)
        def _():
            act(0)

        @pl.when(me > 0)
        def _():
            act(1)

    def send_halo(field, level):
        each_side(field, level, lambda side: halo_copy(field, level, side).start())

    def wait_halo(field, level):
        each_side(field, level, lambda side: halo_copy(field, level, 1 - side).wait_recv())

    def wait_sent(field, level):
        each_side(field, level, lambda side: halo_copy(field, level, side).wait_send())

    @pl.loop(1, devices)
    def _(distance):
        out_copy(lax.rem(me + distance, devices)).start()

    send_halo(RCV, 0)

    own = pl.ds(pl.multiple_of(me * block, 8), block)
    landed[own, :] = staged[own, :]

    row_at = lax.broadcasted_iota(jnp.int32, (cells_x, cells_z), 0)
    lane_at = lax.broadcasted_iota(jnp.int32, (cells_x, cells_z), 1)
    column = ((row_at == shot[0]) & (lane_at == shot[2])).astype(jnp.float32)
    for y in range(slab_y):
        spot[y] = column * (me * slab_y + y == shot[1]).astype(jnp.float32)
    x_at = lax.broadcasted_iota(jnp.int32, (cells_x, traces.shape[2]), 0)
    for y in range(slab_y):
        onehot = (x_at == rec_x[y : y + 1, :]).astype(jnp.float32)
        for step in range(steps):
            total = jnp.sum(onehot * traces[y, step : step + 1, :], axis=1, keepdims=True)
            surface[step, y] = jnp.where(lane_at == 0, total, 0.0)

    def older(field, level, y):
        if level > 0:
            return levels[level - 1, field, REACH + y, inside, :]
        if field == RCV:
            return rcv_old[y]
        return landed[pl.ds(span + y, cells_x, stride=rows), :]

    def local(field, level):
        for y in range(slab_y):
            centre = levels[level, field, REACH + y, inside, :]

            def along_x(shift):
                if shift == 0:
                    return centre
                return levels[level, field, REACH + y, pl.ds(EDGE + shift, cells_x), :]

            def along_z(shift):
                if shift == 0:
                    return centre
                turned = pltpu.roll(centre, (-shift) % cells_z, 1)
                kept = lane_at >= -shift if shift < 0 else lane_at < cells_z - shift
                return jnp.where(kept, turned, 0.0)

            partial[field, y] = (
                2.0 * centre
                - older(field, level, y)
                + medium[0, y] * second(along_x)
                + medium[2, y] * second(along_z)
            )

    def finish(field, level):
        for y in range(slab_y):
            def along_y(shift):
                return levels[level, field, REACH + y + shift, inside, :]

            if field == SRC:
                added = -wavelet[level] * spot[y]
            else:
                added = surface[level, y]
            levels[level + 1, field, REACH + y, inside, :] = (
                partial[field, y] + medium[1, y] * second(along_y) + added
            )

    local(RCV, 0)
    wait_halo(RCV, 0)
    finish(RCV, 0)
    send_halo(RCV, 1)
    local(RCV, 1)

    arrived = landed.at[pl.ds(0, (devices - 1) * block)]
    pltpu.make_async_copy(arrived, arrived, out_recv).wait()
    for y in range(span):
        levels[0, SRC, y, inside, :] = landed[pl.ds(y, cells_x, stride=rows), :]
    local(SRC, 0)
    finish(SRC, 0)
    for level in range(1, steps):
        send_halo(SRC, level)
        local(SRC, level)
        wait_halo(RCV, level)
        finish(RCV, level)
        if level + 1 < steps:
            send_halo(RCV, level + 1)
            local(RCV, level + 1)
        wait_halo(SRC, level)
        finish(SRC, level)

    for back, level in enumerate((steps, steps - 1)):
        for x in range(slab_x):
            for y in range(slab_y):
                at = (back * slab_x + x) * slab_y + y
                leaving[pl.ds(at, devices, stride=back_rows), :] = levels[
                    level, SRC, REACH + y, pl.ds(EDGE + x, devices, stride=slab_x), :
                ]

    def back_copy(peer):
        return pltpu.make_async_remote_copy(
            src_ref=leaving.at[pl.ds(pl.multiple_of(peer * back_rows, 8), back_rows)],
            dst_ref=returned.at[pl.ds(pl.multiple_of(me * back_rows, 8), back_rows)],
            send_sem=back_send,
            recv_sem=back_recv,
            device_id={"wide": peer},
            device_id_type=MESH,
        )

    @pl.loop(1, devices)
    def _(distance):
        back_copy(lax.rem(me + distance, devices)).start()

    own_back = pl.ds(pl.multiple_of(me * back_rows, 8), back_rows)
    returned[own_back, :] = leaving[own_back, :]
    for y in range(slab_y):
        rcv_next[y] = levels[steps, RCV, REACH + y, inside, :]
        rcv_prior[y] = levels[steps - 1, RCV, REACH + y, inside, :]
        for field in (SRC, RCV):
            for snap in range(snaps.shape[0]):
                snaps[snap, field, y] = levels[2 * snap + 2, field, REACH + y, inside, :]

    sent = staged.at[pl.ds(0, (devices - 1) * block)]
    pltpu.make_async_copy(sent, sent, out_send).wait()
    for level in range(steps):
        wait_sent(RCV, level)
        if level > 0:
            wait_sent(SRC, level)

    came = returned.at[pl.ds(0, (devices - 1) * back_rows)]
    pltpu.make_async_copy(came, came, back_recv).wait()
    for back, result in enumerate((src_next, src_prior)):
        for x in range(slab_x):
            for y in range(slab_y):
                at = (back * slab_x + x) * slab_y + y
                result[x, pl.ds(y, devices, stride=slab_y), :] = returned[
                    pl.ds(at, devices, stride=back_rows), :
                ]
    gone = leaving.at[pl.ds(0, (devices - 1) * back_rows)]
    pltpu.make_async_copy(gone, gone, back_send).wait()


def image_kernel(lag_order, snaps, a, b, c, d, a_out, b_out, c_out, d_out, image, padded, board, sems):
    lags = lag_order.shape[0]
    half = (lags - 1) // 2
    taken, fields, slab_y, cells_x, cells_z = snaps.shape
    edge = jnp.zeros((half, cells_z), jnp.float32)
    for snap in range(taken):
        for field in range(fields):
            for y in range(slab_y):
                padded[snap, field, y, 0:half, :] = edge
                padded[snap, field, y, half : half + cells_x, :] = snaps[snap, field, y]
                padded[snap, field, y, half + cells_x : 2 * half + cells_x, :] = edge
    chunk = -(-lags // 3)
    copies = []
    for part, first in enumerate(range(0, lags, chunk)):
        count = min(chunk, lags - first)
        for plane in range(first, first + count):
            slot = lag_order[plane]
            at_src = pl.ds(2 * half - slot, cells_x)
            at_rcv = pl.ds(slot, cells_x)
            for y in range(slab_y):
                total = None
                for snap in range(taken):
                    product = padded[snap, SRC, y, at_src, :] * padded[snap, RCV, y, at_rcv, :]
                    total = product if total is None else total + product
                board[plane, y] = total
        copy = pltpu.make_async_copy(
            board.at[pl.ds(first, count)], image.at[pl.ds(first, count)], sems.at[part]
        )
        copy.start()
        copies.append(copy)
    a_out[...] = a[...]
    b_out[...] = b[...]
    c_out[...] = c[...]
    d_out[...] = d[...]
    for copy in copies:
        copy.wait()


MESH = pl.DeviceIdType.MESH


def solution(mesh):
    devices = mesh.shape["wide"]

    def on_device(
        src_now, src_old, rcv_now, rcv_old, medium, wavelet, shot, traces, rec_x, lag_order
    ):
        slab_x, cells_y, cells_z = src_now.shape
        slab_y, _, cells_x = rcv_now.shape
        steps = wavelet.shape[0]
        lags = lag_order.shape[0]
        half = (lags - 1) // 2
        span = slab_y + 2 * REACH
        rows = -(-(span + slab_y) // 8) * 8
        f32 = jnp.float32
        vmem = pl.BlockSpec(memory_space=pltpu.VMEM)
        smem = pl.BlockSpec(memory_space=pltpu.SMEM)
        src_shape = jax.ShapeDtypeStruct((slab_x, cells_y, cells_z), f32)
        rcv_shape = jax.ShapeDtypeStruct((slab_y, cells_x, cells_z), f32)
        taken = steps // 2
        turn = lambda array: jnp.swapaxes(array, -1, -2)
        src_next, src_prior, rcv_next, rcv_prior, snaps = pl.pallas_call(
            functools.partial(window_kernel, devices),
            out_shape=(
                src_shape,
                src_shape,
                rcv_shape,
                rcv_shape,
                jax.ShapeDtypeStruct((taken, 2, slab_y, cells_x, cells_z), f32),
            ),
            in_specs=[vmem] * 5 + [smem] * 2 + [vmem] * 2,
            out_specs=(vmem,) * 5,
            scratch_shapes=[
                pltpu.VMEM((cells_x * rows, cells_z), f32),
                pltpu.VMEM((cells_x * rows, cells_z), f32),
                pltpu.VMEM((steps + 1, 2, span, cells_x + 2 * EDGE, cells_z), f32),
                pltpu.VMEM((2, slab_y, cells_x, cells_z), f32),
                pltpu.VMEM((steps, slab_y, cells_x, cells_z), f32),
                pltpu.VMEM((slab_y, cells_x, cells_z), f32),
                pltpu.VMEM((devices * 2 * slab_x * slab_y, cells_z), f32),
                pltpu.VMEM((devices * 2 * slab_x * slab_y, cells_z), f32),
                pltpu.SemaphoreType.DMA,
                pltpu.SemaphoreType.DMA,
                pltpu.SemaphoreType.DMA,
                pltpu.SemaphoreType.DMA,
                pltpu.SemaphoreType.DMA((2, steps, 2)),
                pltpu.SemaphoreType.DMA((2, steps, 2)),
            ],
            compiler_params=pltpu.CompilerParams(collective_id=0, has_side_effects=True),
            name="window",
        )(
            src_now,
            src_old,
            turn(rcv_now),
            turn(rcv_old),
            turn(medium),
            wavelet,
            shot,
            turn(traces),
            rec_x,
        )
        outs = pl.pallas_call(
            image_kernel,
            out_shape=(
                src_shape,
                src_shape,
                rcv_shape,
                rcv_shape,
                jax.ShapeDtypeStruct((lags, slab_y, cells_x, cells_z), f32),
            ),
            in_specs=[smem] + [vmem] * 5,
            out_specs=(vmem,) * 4 + (pl.BlockSpec(memory_space=pl.ANY),),
            scratch_shapes=[
                pltpu.VMEM((taken, 2, slab_y, cells_x + 2 * half, cells_z), f32),
                pltpu.VMEM((lags, slab_y, cells_x, cells_z), f32),
                pltpu.SemaphoreType.DMA((3,)),
            ],
            name="image",
        )(lag_order, snaps, src_next, src_prior, rcv_next, rcv_prior)
        return outs[0], outs[1], turn(outs[2]), turn(outs[3]), turn(outs[4])

    return jax.shard_map(
        on_device,
        mesh=mesh,
        in_specs=(
            P("wide", "shots", None),
            P("wide", "shots", None),
            P("wide", "shots", None),
            P("wide", "shots", None),
            P(None, "wide", None, None),
            P(),
            P("shots"),
            P("wide", "shots", None),
            P("wide", "shots"),
            P(),
        ),
        out_specs=(
            P("wide", "shots", None),
            P("wide", "shots", None),
            P("wide", "shots", None),
            P("wide", "shots", None),
            P("shots", "wide", None, None),
        ),
        check_vma=False,
    )
```

time: 224 us -> 28.8 us (0.13); the launches traced: 220 us -> 28.7 us
  loops' own time: 85 us -> 0 us
  local copies, waits for them, and re-layouts: 67.3 us -> 0 us
  starting transfers between devices: 47 us -> 0 us
  Pallas kernels: 0 us -> 28 us
  waiting for transfers between devices: 10.6 us -> 0 us
  other arithmetic: 5.48 us -> 0 us
  between operations: 3.54 us -> 0.64 us
    another operation x1 -> x0, loops' own time: 85 us -> none  [lagged(): return lax.map(one_plane, lag_order)]
    dynamic_slice x231 -> x0, local copies, waits for them, and re-layouts: 34.2 us -> none  [the longest x33 19.9 us: lagged(): return lax.map(one_plane, lag_order)]
    pallas_call x0 -> x2, Pallas kernels: none -> 28 us  [the longest x1 25.3 us: on_device(): pl.pallas_call(functools.partial(window_kernel, devices), out_shape=(src_...]
    all_to_all x4 -> x0, starting transfers between devices: 24.3 us -> none  [the longest x1 7.41 us: on_device(): lax.all_to_all(pair_old[0], 'wide', split_axis=2, concat_axis=0, tiled=True)]
    dynamic_update_slice x66 -> x0, local copies, waits for them, and re-layouts: 23 us -> none  [lagged(): return lax.map(one_plane, lag_order)]
    ppermute x8 -> x0, starting transfers between devices: 22.7 us -> none  [the longest x4 17.5 us: extended(): before = lax.ppermute(last, axis, up)]
    all_to_all x4 -> x0, waiting for transfers between devices: 8.17 us -> none  [the longest x1 6.59 us: on_device(): lax.all_to_all(pair_old[0], 'wide', split_axis=2, concat_axis=0, tiled=True)]
    unnamed x12 -> x0, local copies, waits for them, and re-layouts: 2.84 us -> none
  transfers between devices with their start and end apart: 12 -> 0, of which waited for: 5 -> 0; matrix products, arithmetic and copies ran while one was open for 31% -> 0% of each run, Pallas kernels for 0% -> 0%
where the time goes in v1:
time: 28.8 us; the launch traced here: 28.7 us
  Pallas kernels  28 us (97%)
  between operations  0.64 us (2%)
    pallas_call x1, Pallas kernels, on_device(): pl.pallas_call(functools.partial(window_kernel, devices), out_shape=(src_...  25.3 us
    pallas_call x1, Pallas kernels, on_device(): pl.pallas_call(image_kernel, out_shape=(src_shape, src_shape, rcv_shape,...  2.71 us

profile of v1, /device:TPU:0, one launch (start us, length us, event | category | flops | bytes accessed | tf_op | source)
XLA Modules:
  0.0 28.7 jit_solution(17586883381468824479)
XLA Ops:
  0.6 25.3 %window.1 = (f32[2,32,128]{2,1,0:T(8,128)}, f32[2,32,128]{2,1,0:T(8,128)}, f32[2,32,128]{2,1,0:T(8,128)}, f32[2,32,128]{2,1,0:T(8,128)}, f32[2,2,2,32,128]{4,3,2,1,0:T(8,128)}) custom-call(f32[2,32,128]{2,1,0:T(8,128)} %src_now.1, f32[2,32,128]{2,1,0:T(8,128)} %src_old.1, f32[2,32,128]{2,1,0:T(8,128)} %bitcast.8, f32[2,32,128]{2,1,0:T(8,128)} %bitcast.9, ...), custom_call_target="tpu_custom_call" | custom-call | tf_op jit(solution)/shard_map/window/pallas_call | solution.py:358
  26.0 2.7 %image.1 = (f32[2,32,128]{2,1,0:T(8,128)}, f32[2,32,128]{2,1,0:T(8,128)}, f32[2,32,128]{2,1,0:T(8,128)}, f32[2,32,128]{2,1,0:T(8,128)}, f32[33,2,32,128]{3,2,1,0:T(8,128)}) custom-call(s32[33]{0:T(128)} %lag_order.1, f32[2,2,2,32,128]{4,3,2,1,0:T(8,128)} %get-tuple-element.15.snaps, f32[2,32,128]{2,1,0:T(8,128)} %get-tuple-element.16.a, ...), custom_call_target="tpu_custom_call" | custom-call | tf_op jit(solution)/shard_map/image/pallas_call | solution.py:398

commit v2 on v1

v2 whole, which is shorter than its diff:
```python
import functools
import math

import jax
import jax.numpy as jnp
from jax import lax
from jax.experimental import pallas as pl
from jax.experimental.pallas import tpu as pltpu
from jax.sharding import PartitionSpec as P

REACH = 2
EDGE = 8
OUTER, INNER, CENTRE = -1.0 / 12.0, 4.0 / 3.0, -2.5
SRC, RCV = 0, 1


def second(window):
    return (
        OUTER * (window(-2) + window(2)) + INNER * (window(-1) + window(1)) + CENTRE * window(0)
    )


def window_kernel(
    devices,
    src_now_in,
    src_old_in,
    rcv_now_in,
    rcv_old_in,
    medium_in,
    wavelet_in,
    shot_in,
    traces_in,
    rec_x_in,
    lag_order_in,
    src_next,
    src_prior,
    rcv_next,
    rcv_prior,
    board,
    src_now,
    src_old,
    rcv_old,
    medium,
    wavelet,
    shot,
    traces,
    rec_x,
    lag_order,
    padded,
    staged,
    landed,
    levels,
    partial,
    surface,
    spot,
    leaving,
    returned,
    out_send,
    out_recv,
    back_send,
    back_recv,
    halo_send,
    halo_recv,
    load_sems,
):
    me = lax.axis_index("wide")
    slab_x, cells_y, cells_z = src_now.shape
    slab_y, cells_x, _ = rcv_old.shape
    steps = wavelet.shape[0]
    span = slab_y + 2 * REACH
    rows = staged.shape[0] // (devices * slab_x)
    block = slab_x * rows
    back_rows = 2 * slab_x * slab_y
    inside = pl.ds(EDGE, cells_x)

    lags = lag_order.shape[0]
    half = (lags - 1) // 2
    middle = devices // 2
    far_first = sorted(range(1, devices), key=lambda distance: abs(distance - middle))

    loads = []
    for index, (source, target) in enumerate(
        (
            (src_now_in, src_now),
            (src_old_in, src_old),
            (rcv_now_in, levels.at[0, RCV, pl.ds(REACH, slab_y), inside]),
            (shot_in, shot),
            (traces_in, traces),
            (rec_x_in, rec_x),
            (rcv_old_in, rcv_old),
            (medium_in, medium),
            (wavelet_in, wavelet),
            (lag_order_in, lag_order),
        )
    ):
        loads.append(pltpu.make_async_copy(source, target, load_sems.at[index]))
    for load in loads[:3]:
        load.start()

    barrier = pltpu.get_barrier_semaphore()
    for distance in far_first:
        pl.semaphore_signal(
            barrier,
            inc=1,
            device_id={"wide": lax.rem(me + distance, devices)},
            device_id_type=MESH,
        )
    for load in loads[3:]:
        load.start()

    zero_edge = jnp.zeros((EDGE, cells_z), jnp.float32)
    zero_plane = jnp.zeros((cells_x, cells_z), jnp.float32)
    zero_half = jnp.zeros((half, cells_z), jnp.float32)
    for snap in range(padded.shape[0]):
        for field in (SRC, RCV):
            for y in range(slab_y):
                padded[snap, field, y, 0:half, :] = zero_half
                padded[snap, field, y, half + cells_x : 2 * half + cells_x, :] = zero_half
    for level in range(steps):
        for field in (SRC, RCV):
            for y in range(REACH, REACH + slab_y):
                levels[level, field, y, 0:EDGE, :] = zero_edge
                levels[level, field, y, EDGE + cells_x : EDGE + cells_x + EDGE, :] = zero_edge

    @pl.when(me == 0)
    def _():
        for level in range(steps):
            for field in (SRC, RCV):
                for y in range(REACH):
                    levels[level, field, y, inside, :] = zero_plane

    @pl.when(me == devices - 1)
    def _():
        for level in range(steps):
            for field in (SRC, RCV):
                for y in range(REACH):
                    levels[level, field, REACH + slab_y + y, inside, :] = zero_plane

    loads[0].wait()
    loads[1].wait()

    for peer in range(devices):
        first = peer * slab_y - REACH
        low, high = max(first, 0), min(first + span, cells_y)
        for x in range(slab_x):
            base = (peer * slab_x + x) * rows
            if low > first or high < first + span:
                staged[base : base + rows, :] = jnp.zeros((rows, cells_z), jnp.float32)
            staged[base + low - first : base + high - first, :] = src_now[x, low:high, :]
            staged[base + span : base + span + slab_y, :] = src_old[
                x, peer * slab_y : (peer + 1) * slab_y, :
            ]

    for load in loads[3:]:
        load.wait()
    row_at = lax.broadcasted_iota(jnp.int32, (cells_x, cells_z), 0)
    lane_at = lax.broadcasted_iota(jnp.int32, (cells_x, cells_z), 1)
    column = ((row_at == shot[0]) & (lane_at == shot[2])).astype(jnp.float32)
    for y in range(slab_y):
        spot[y] = column * (me * slab_y + y == shot[1]).astype(jnp.float32)
    x_at = lax.broadcasted_iota(jnp.int32, (cells_x, traces.shape[2]), 0)
    for y in range(slab_y):
        onehot = (x_at == rec_x[y : y + 1, :]).astype(jnp.float32)
        for step in range(steps):
            total = jnp.sum(onehot * traces[y, step : step + 1, :], axis=1, keepdims=True)
            surface[step, y] = jnp.where(lane_at == 0, total, 0.0)
    loads[2].wait()

    pl.semaphore_wait(barrier, devices - 1)

    def out_copy(peer):
        return pltpu.make_async_remote_copy(
            src_ref=staged.at[pl.ds(pl.multiple_of(peer * block, 8), block)],
            dst_ref=landed.at[pl.ds(pl.multiple_of(me * block, 8), block)],
            send_sem=out_send,
            recv_sem=out_recv,
            device_id={"wide": peer},
            device_id_type=MESH,
        )

    def halo_copy(field, level, side):
        first = slab_y if side == 0 else REACH
        source = levels.at[level, field, pl.ds(first, REACH), inside]
        into = 0 if side == 0 else REACH + slab_y
        peer = me + 1 if side == 0 else me - 1
        return pltpu.make_async_remote_copy(
            src_ref=source,
            dst_ref=levels.at[level, field, pl.ds(into, REACH), inside],
            send_sem=halo_send.at[field, level, side],
            recv_sem=halo_recv.at[field, level, side],
            device_id={"wide": peer},
            device_id_type=MESH,
        )

    def each_side(field, level, act):
        @pl.when(me < devices - 1)
        def _():
            act(0)

        @pl.when(me > 0)
        def _():
            act(1)

    def send_halo(field, level):
        each_side(field, level, lambda side: halo_copy(field, level, side).start())

    def wait_halo(field, level):
        each_side(field, level, lambda side: halo_copy(field, level, 1 - side).wait_recv())

    def wait_sent(field, level):
        each_side(field, level, lambda side: halo_copy(field, level, side).wait_send())

    for distance in far_first:
        out_copy(lax.rem(me + distance, devices)).start()

    send_halo(RCV, 0)

    own = pl.ds(pl.multiple_of(me * block, 8), block)
    landed[own, :] = staged[own, :]

    def older(field, level, y):
        if level > 0:
            return levels[level - 1, field, REACH + y, inside, :]
        if field == RCV:
            return rcv_old[y]
        return landed[pl.ds(span + y, cells_x, stride=rows), :]

    def local(field, level):
        for y in range(slab_y):
            centre = levels[level, field, REACH + y, inside, :]

            def along_x(shift):
                if shift == 0:
                    return centre
                return levels[level, field, REACH + y, pl.ds(EDGE + shift, cells_x), :]

            def along_z(shift):
                if shift == 0:
                    return centre
                turned = pltpu.roll(centre, (-shift) % cells_z, 1)
                kept = lane_at >= -shift if shift < 0 else lane_at < cells_z - shift
                return jnp.where(kept, turned, 0.0)

            partial[field, y] = (
                2.0 * centre
                - older(field, level, y)
                + medium[0, y] * second(along_x)
                + medium[2, y] * second(along_z)
            )

    def finish(field, level):
        for y in range(slab_y):
            def along_y(shift):
                return levels[level, field, REACH + y + shift, inside, :]

            if field == SRC:
                added = -wavelet[level] * spot[y]
            else:
                added = surface[level, y]
            levels[level + 1, field, REACH + y, inside, :] = (
                partial[field, y] + medium[1, y] * second(along_y) + added
            )

    local(RCV, 0)
    wait_halo(RCV, 0)
    finish(RCV, 0)
    send_halo(RCV, 1)
    local(RCV, 1)

    arrived = landed.at[pl.ds(0, (devices - 1) * block)]
    pltpu.make_async_copy(arrived, arrived, out_recv).wait()
    for y in range(span):
        levels[0, SRC, y, inside, :] = landed[pl.ds(y, cells_x, stride=rows), :]
    local(SRC, 0)
    finish(SRC, 0)
    for level in range(1, steps):
        send_halo(SRC, level)
        local(SRC, level)
        wait_halo(RCV, level)
        finish(RCV, level)
        if level + 1 < steps:
            send_halo(RCV, level + 1)
            local(RCV, level + 1)
        wait_halo(SRC, level)
        finish(SRC, level)

    for back, level in enumerate((steps, steps - 1)):
        for x in range(slab_x):
            for y in range(slab_y):
                at = (back * slab_x + x) * slab_y + y
                leaving[pl.ds(at, devices, stride=back_rows), :] = levels[
                    level, SRC, REACH + y, pl.ds(EDGE + x, devices, stride=slab_x), :
                ]

    def back_copy(peer):
        return pltpu.make_async_remote_copy(
            src_ref=leaving.at[pl.ds(pl.multiple_of(peer * back_rows, 8), back_rows)],
            dst_ref=returned.at[pl.ds(pl.multiple_of(me * back_rows, 8), back_rows)],
            send_sem=back_send,
            recv_sem=back_recv,
            device_id={"wide": peer},
            device_id_type=MESH,
        )

    for distance in far_first:
        back_copy(lax.rem(me + distance, devices)).start()

    own_back = pl.ds(pl.multiple_of(me * back_rows, 8), back_rows)
    returned[own_back, :] = leaving[own_back, :]
    for y in range(slab_y):
        rcv_next[y] = levels[steps, RCV, REACH + y, inside, :]
        rcv_prior[y] = levels[steps - 1, RCV, REACH + y, inside, :]
        for field in (SRC, RCV):
            for snap in range(padded.shape[0]):
                padded[snap, field, y, half : half + cells_x, :] = levels[
                    2 * snap + 2, field, REACH + y, inside, :
                ]
    for plane in range(lags):
        slot = lag_order[plane]
        at_src = pl.ds(2 * half - slot, cells_x)
        at_rcv = pl.ds(slot, cells_x)
        for y in range(slab_y):
            total = None
            for snap in range(padded.shape[0]):
                product = padded[snap, SRC, y, at_src, :] * padded[snap, RCV, y, at_rcv, :]
                total = product if total is None else total + product
            board[plane, y] = total

    sent = staged.at[pl.ds(0, (devices - 1) * block)]
    pltpu.make_async_copy(sent, sent, out_send).wait()
    for level in range(steps):
        wait_sent(RCV, level)
        if level > 0:
            wait_sent(SRC, level)

    came = returned.at[pl.ds(0, (devices - 1) * back_rows)]
    pltpu.make_async_copy(came, came, back_recv).wait()
    for back, result in enumerate((src_next, src_prior)):
        for x in range(slab_x):
            for y in range(slab_y):
                at = (back * slab_x + x) * slab_y + y
                result[x, pl.ds(y, devices, stride=slab_y), :] = returned[
                    pl.ds(at, devices, stride=back_rows), :
                ]
    gone = leaving.at[pl.ds(0, (devices - 1) * back_rows)]
    pltpu.make_async_copy(gone, gone, back_send).wait()


def deliver_kernel(*refs):
    count = (len(refs) - 1) // 2
    copies = [
        pltpu.make_async_copy(refs[i], refs[count + i], refs[-1].at[i]) for i in range(count)
    ]
    for copy in copies:
        copy.start()
    for copy in copies:
        copy.wait()


MESH = pl.DeviceIdType.MESH


def solution(mesh):
    devices = mesh.shape["wide"]

    def on_device(
        src_now, src_old, rcv_now, rcv_old, medium, wavelet, shot, traces, rec_x, lag_order
    ):
        slab_x, cells_y, cells_z = src_now.shape
        slab_y, _, cells_x = rcv_now.shape
        steps = wavelet.shape[0]
        lags = lag_order.shape[0]
        half = (lags - 1) // 2
        span = slab_y + 2 * REACH
        rows = -(-(span + slab_y) // 8) * 8
        f32 = jnp.float32
        vmem = pl.BlockSpec(memory_space=pltpu.VMEM)
        hbm = pl.BlockSpec(memory_space=pltpu.HBM)
        src_shape = jax.ShapeDtypeStruct((slab_x, cells_y, cells_z), f32)
        rcv_shape = jax.ShapeDtypeStruct((slab_y, cells_x, cells_z), f32)
        board_shape = jax.ShapeDtypeStruct((lags, slab_y, cells_x, cells_z), f32)
        shapes = (src_shape, src_shape, rcv_shape, rcv_shape, board_shape)
        taken = steps // 2
        turn = lambda array: jnp.swapaxes(array, -1, -2)
        like = lambda array: pltpu.VMEM(array.shape, array.dtype)
        scalars = lambda array: pltpu.SMEM(array.shape, array.dtype)
        rcv_now, rcv_old, medium, traces = map(turn, (rcv_now, rcv_old, medium, traces))
        scratch = [
            like(src_now),
            like(src_old),
            like(rcv_old),
            like(medium),
            scalars(wavelet),
            scalars(shot),
            like(traces),
            like(rec_x),
            scalars(lag_order),
            pltpu.VMEM((taken, 2, slab_y, cells_x + 2 * half, cells_z), f32),
            pltpu.VMEM((cells_x * rows, cells_z), f32),
            pltpu.VMEM((cells_x * rows, cells_z), f32),
            pltpu.VMEM((steps + 1, 2, span, cells_x + 2 * EDGE, cells_z), f32),
            pltpu.VMEM((2, slab_y, cells_x, cells_z), f32),
            pltpu.VMEM((steps, slab_y, cells_x, cells_z), f32),
            pltpu.VMEM((slab_y, cells_x, cells_z), f32),
            pltpu.VMEM((devices * 2 * slab_x * slab_y, cells_z), f32),
            pltpu.VMEM((devices * 2 * slab_x * slab_y, cells_z), f32),
        ]
        held = sum(4 * math.prod(each.shape) for each in scratch + list(shapes))
        results = pl.pallas_call(
            functools.partial(window_kernel, devices),
            out_shape=shapes,
            in_specs=[hbm] * 10,
            out_specs=(vmem,) * 5,
            scratch_shapes=scratch
            + [pltpu.SemaphoreType.DMA] * 4
            + [
                pltpu.SemaphoreType.DMA((2, steps, 2)),
                pltpu.SemaphoreType.DMA((2, steps, 2)),
                pltpu.SemaphoreType.DMA((10,)),
            ],
            compiler_params=pltpu.CompilerParams(
                collective_id=0, has_side_effects=True, vmem_limit_bytes=held + (4 << 20)
            ),
            name="window",
        )(
            *(
                pltpu.with_memory_space_constraint(array, pltpu.HBM)
                for array in (
                    src_now,
                    src_old,
                    rcv_now,
                    rcv_old,
                    medium,
                    wavelet,
                    shot,
                    traces,
                    rec_x,
                    lag_order,
                )
            )
        )
        outs = pl.pallas_call(
            deliver_kernel,
            out_shape=shapes,
            in_specs=[vmem] * 5,
            out_specs=(hbm,) * 5,
            scratch_shapes=[pltpu.SemaphoreType.DMA((5,))],
            compiler_params=pltpu.CompilerParams(vmem_limit_bytes=held + (4 << 20)),
            name="deliver",
        )(*results)
        return outs[0], outs[1], turn(outs[2]), turn(outs[3]), turn(outs[4])

    return jax.shard_map(
        on_device,
        mesh=mesh,
        in_specs=(
            P("wide", "shots", None),
            P("wide", "shots", None),
            P("wide", "shots", None),
            P("wide", "shots", None),
            P(None, "wide", None, None),
            P(),
            P("shots"),
            P("wide", "shots", None),
            P("wide", "shots"),
            P(),
        ),
        out_specs=(
            P("wide", "shots", None),
            P("wide", "shots", None),
            P("wide", "shots", None),
            P("wide", "shots", None),
            P("shots", "wide", None, None),
        ),
        check_vma=False,
    )
```

time: 28.8 us -> 25.5 us (0.89)
  Pallas kernels: 28 us -> 24.7 us
    pallas_call x2, Pallas kernels: 28 us -> 24.7 us  [the longest x1 23.6 us: on_device(): pl.pallas_call(functools.partial(window_kernel, devices), out_shape=shape...]
where the time goes in v2:
time: 25.5 us; the launch traced here: 25.3 us
  Pallas kernels  24.7 us (97%)
  between operations  0.64 us (3%)
    pallas_call x1, Pallas kernels, on_device(): pl.pallas_call(functools.partial(window_kernel, devices), out_shape=shape...  23.6 us
    pallas_call x1, Pallas kernels, on_device(): pl.pallas_call(deliver_kernel, out_shape=shapes, in_specs=[vmem] * 5, out...  1.07 us

profile of v2, /device:TPU:0, one launch (start us, length us, event | category | flops | bytes accessed | tf_op | source)
XLA Modules:
  0.0 25.3 jit_solution(11156499057668812402)
XLA Ops:
  0.6 23.6 %window.1 = (f32[2,32,128]{2,1,0:T(8,128)S(1)}, f32[2,32,128]{2,1,0:T(8,128)S(1)}, f32[2,32,128]{2,1,0:T(8,128)S(1)}, f32[2,32,128]{2,1,0:T(8,128)S(1)}, f32[33,2,32,128]{3,2,1,0:T(8,128)S(1)}) custom-call(f32[2,32,128]{2,1,0:T(8,128)} %src_now_in.1, f32[2,32,128]{2,1,0:T(8,128)} %src_old_in.1, f32[2,32,128]{2,1,0:T(8,128)} %bitcast.8, ...), custom_call_target="tpu_custom_call" | custom-call | tf_op jit(solution)/shard_map/window/pallas_call | solution.py:409
  24.3 1.1 %deliver.1 = (f32[2,32,128]{2,1,0:T(8,128)}, f32[2,32,128]{2,1,0:T(8,128)}, f32[2,32,128]{2,1,0:T(8,128)}, f32[2,32,128]{2,1,0:T(8,128)}, f32[33,2,32,128]{3,2,1,0:T(8,128)}) custom-call(f32[2,32,128]{2,1,0:T(8,128)S(1)} %get-tuple-element.15.refs_0_, f32[2,32,128]{2,1,0:T(8,128)S(1)} %get-tuple-element.16.refs_1_, ...), custom_call_target="tpu_custom_call" | custom-call | tf_op jit(solution)/shard_map/deliver/pallas_call | solution.py:442

commit v3 on v2

--- a/solution.py
+++ b/solution.py
@@ -62,12 +62,15 @@
     halo_send,
     halo_recv,
     load_sems,
+    side_send,
+    side_recv,
 ):
     me = lax.axis_index("wide")
     slab_x, cells_y, cells_z = src_now.shape
     slab_y, cells_x, _ = rcv_old.shape
     steps = wavelet.shape[0]
     span = slab_y + 2 * REACH
+    pad = 2 * REACH
     rows = staged.shape[0] // (devices * slab_x)
     block = slab_x * rows
     back_rows = 2 * slab_x * slab_y
@@ -83,12 +86,12 @@
         (
             (src_now_in, src_now),
             (src_old_in, src_old),
-            (rcv_now_in, levels.at[0, RCV, pl.ds(REACH, slab_y), inside]),
+            (rcv_now_in, levels.at[0, RCV, pl.ds(pad, slab_y), inside]),
             (shot_in, shot),
             (traces_in, traces),
             (rec_x_in, rec_x),
             (rcv_old_in, rcv_old),
-            (medium_in, medium),
+            (medium_in, medium.at[:, pl.ds(REACH, slab_y)]),
             (wavelet_in, wavelet),
             (lag_order_in, lag_order),
         )
@@ -118,23 +121,22 @@
                 padded[snap, field, y, half + cells_x : 2 * half + cells_x, :] = zero_half
     for level in range(steps):
         for field in (SRC, RCV):
-            for y in range(REACH, REACH + slab_y):
+            for y in range(REACH, REACH + span):
                 levels[level, field, y, 0:EDGE, :] = zero_edge
                 levels[level, field, y, EDGE + cells_x : EDGE + cells_x + EDGE, :] = zero_edge
 
-    @pl.when(me == 0)
-    def _():
-        for level in range(steps):
-            for field in (SRC, RCV):
-                for y in range(REACH):
-                    levels[level, field, y, inside, :] = zero_plane
-
-    @pl.when(me == devices - 1)
-    def _():
-        for level in range(steps):
-            for field in (SRC, RCV):
-                for y in range(REACH):
-                    levels[level, field, REACH + slab_y + y, inside, :] = zero_plane
+    def clear(near, planes):
+        @pl.when(near)
+        def _():
+            for level in range(steps):
+                for field in (SRC, RCV):
+                    for plane in planes:
+                        levels[level, field, plane, inside, :] = zero_plane
+
+    clear(me < 2, range(REACH))
+    clear(me < 1, range(REACH, pad))
+    clear(me >= devices - 2, range(pad + 2 * slab_y, 2 * pad + slab_y))
+    clear(me >= devices - 1, range(pad + slab_y, pad + 2 * slab_y))
 
     loads[0].wait()
     loads[1].wait()
@@ -156,14 +158,14 @@
     row_at = lax.broadcasted_iota(jnp.int32, (cells_x, cells_z), 0)
     lane_at = lax.broadcasted_iota(jnp.int32, (cells_x, cells_z), 1)
     column = ((row_at == shot[0]) & (lane_at == shot[2])).astype(jnp.float32)
-    for y in range(slab_y):
-        spot[y] = column * (me * slab_y + y == shot[1]).astype(jnp.float32)
+    for y in range(-REACH, slab_y + REACH):
+        spot[REACH + y] = column * (me * slab_y + y == shot[1]).astype(jnp.float32)
     x_at = lax.broadcasted_iota(jnp.int32, (cells_x, traces.shape[2]), 0)
     for y in range(slab_y):
         onehot = (x_at == rec_x[y : y + 1, :]).astype(jnp.float32)
         for step in range(steps):
             total = jnp.sum(onehot * traces[y, step : step + 1, :], axis=1, keepdims=True)
-            surface[step, y] = jnp.where(lane_at == 0, total, 0.0)
+            surface[step, REACH + y] = jnp.where(lane_at == 0, total, 0.0)
     loads[2].wait()
 
     pl.semaphore_wait(barrier, devices - 1)
@@ -178,61 +180,92 @@
             device_id_type=MESH,
         )
 
-    def halo_copy(field, level, side):
-        first = slab_y if side == 0 else REACH
-        source = levels.at[level, field, pl.ds(first, REACH), inside]
-        into = 0 if side == 0 else REACH + slab_y
-        peer = me + 1 if side == 0 else me - 1
+    def send_to(hop, side, source, target, send_sem, recv_sem):
         return pltpu.make_async_remote_copy(
             src_ref=source,
-            dst_ref=levels.at[level, field, pl.ds(into, REACH), inside],
-            send_sem=halo_send.at[field, level, side],
-            recv_sem=halo_recv.at[field, level, side],
-            device_id={"wide": peer},
+            dst_ref=target,
+            send_sem=send_sem,
+            recv_sem=recv_sem,
+            device_id={"wide": me + hop if side == 0 else me - hop},
             device_id_type=MESH,
         )
 
-    def each_side(field, level, act):
-        @pl.when(me < devices - 1)
+    def halo_copy(field, level, hop, side):
+        into = pad - hop * slab_y if side == 0 else pad + hop * slab_y
+        return send_to(
+            hop,
+            side,
+            levels.at[level, field, pl.ds(pad, slab_y), inside],
+            levels.at[level, field, pl.ds(into, slab_y), inside],
+            halo_send.at[field, level, hop - 1, side],
+            halo_recv.at[field, level, hop - 1, side],
+        )
+
+    def side_copy(kind, side):
+        into = pl.ds(0 if side == 0 else REACH + slab_y, slab_y)
+        whole = medium if kind == 0 else surface
+        lead = pl.ds(0, 3) if kind == 0 else pl.ds(1, steps - 3)
+        return send_to(
+            1,
+            side,
+            whole.at[lead, pl.ds(REACH, slab_y)],
+            whole.at[lead, into],
+            side_send.at[kind, side],
+            side_recv.at[kind, side],
+        )
+
+    def each_side(hop, act):
+        @pl.when(me < devices - hop)
         def _():
             act(0)
 
-        @pl.when(me > 0)
+        @pl.when(me >= hop)
         def _():
             act(1)
 
-    def send_halo(field, level):
-        each_side(field, level, lambda side: halo_copy(field, level, side).start())
-
-    def wait_halo(field, level):
-        each_side(field, level, lambda side: halo_copy(field, level, 1 - side).wait_recv())
-
-    def wait_sent(field, level):
-        each_side(field, level, lambda side: halo_copy(field, level, side).wait_send())
+    def wide(level):
+        return level % 2 == 1 and level + 1 < steps
+
+    def hops(level):
+        return (1, 2) if wide(level) else (1,) if level % 2 == 1 else ()
+
+    def send_halo(field, level, reach):
+        for hop in reach:
+            each_side(hop, lambda side: halo_copy(field, level, hop, side).start())
+
+    def wait_halo(field, level, reach):
+        for hop in reach:
+            each_side(hop, lambda side: halo_copy(field, level, hop, 1 - side).wait_recv())
+
+    def wait_sent(field, level, reach):
+        for hop in reach:
+            each_side(hop, lambda side: halo_copy(field, level, hop, side).wait_send())
 
     for distance in far_first:
         out_copy(lax.rem(me + distance, devices)).start()
 
-    send_halo(RCV, 0)
+    send_halo(RCV, 0, (1,))
+    for kind in range(2):
+        each_side(1, lambda side: side_copy(kind, side).start())
 
     own = pl.ds(pl.multiple_of(me * block, 8), block)
     landed[own, :] = staged[own, :]
 
     def older(field, level, y):
         if level > 0:
-            return levels[level - 1, field, REACH + y, inside, :]
+            return levels[level - 1, field, pad + y, inside, :]
         if field == RCV:
             return rcv_old[y]
         return landed[pl.ds(span + y, cells_x, stride=rows), :]
 
-    def local(field, level):
-        for y in range(slab_y):
-            centre = levels[level, field, REACH + y, inside, :]
+    def local(field, level, planes):
+        for y in planes:
+            centre = levels[level, field, pad + y, inside, :]
 
             def along_x(shift):
                 if shift == 0:
                     return centre
-                return levels[level, field, REACH + y, pl.ds(EDGE + shift, cells_x), :]
+                return levels[level, field, pad + y, pl.ds(EDGE + shift, cells_x), :]
 
             def along_z(shift):
                 if shift == 0:
@@ -241,55 +274,72 @@
                 kept = lane_at >= -shift if shift < 0 else lane_at < cells_z - shift
                 return jnp.where(kept, turned, 0.0)
 
-            partial[field, y] = (
+            partial[field, REACH + y] = (
                 2.0 * centre
                 - older(field, level, y)
-                + medium[0, y] * second(along_x)
-                + medium[2, y] * second(along_z)
+                + medium[0, REACH + y] * second(along_x)
+                + medium[2, REACH + y] * second(along_z)
             )
 
-    def finish(field, level):
-        for y in range(slab_y):
+    def finish(field, level, planes):
+        for y in planes:
             def along_y(shift):
-                return levels[level, field, REACH + y + shift, inside, :]
+                return levels[level, field, pad + y + shift, inside, :]
 
             if field == SRC:
-                added = -wavelet[level] * spot[y]
+                added = -wavelet[level] * spot[REACH + y]
             else:
-                added = surface[level, y]
-            levels[level + 1, field, REACH + y, inside, :] = (
-                partial[field, y] + medium[1, y] * second(along_y) + added
+                added = surface[level, REACH + y]
+            levels[level + 1, field, pad + y, inside, :] = (
+                partial[field, REACH + y] + medium[1, REACH + y] * second(along_y) + added
             )
 
-    local(RCV, 0)
-    wait_halo(RCV, 0)
-    finish(RCV, 0)
-    send_halo(RCV, 1)
-    local(RCV, 1)
+    mine = range(slab_y)
+
+    def around(field, level):
+        def act(side):
+            planes = range(slab_y, slab_y + REACH) if side == 0 else range(-REACH, 0)
+            local(field, level, planes)
+            finish(field, level, planes)
+
+        each_side(1, act)
+
+    local(RCV, 0, mine)
+    wait_halo(RCV, 0, (1,))
+    finish(RCV, 0, mine)
+    send_halo(RCV, 1, hops(1))
+    local(RCV, 1, mine)
 
     arrived = landed.at[pl.ds(0, (devices - 1) * block)]
     pltpu.make_async_copy(arrived, arrived, out_recv).wait()
     for y in range(span):
-        levels[0, SRC, y, inside, :] = landed[pl.ds(y, cells_x, stride=rows), :]
-    local(SRC, 0)
-    finish(SRC, 0)
+        levels[0, SRC, REACH + y, inside, :] = landed[pl.ds(y, cells_x, stride=rows), :]
+    local(SRC, 0, mine)
+    finish(SRC, 0, mine)
     for level in range(1, steps):
-        send_halo(SRC, level)
-        local(SRC, level)
-        wait_halo(RCV, level)
-        finish(RCV, level)
+        send_halo(SRC, level, hops(level))
+        local(SRC, level, mine)
+        wait_halo(RCV, level, hops(level))
+        finish(RCV, level, mine)
         if level + 1 < steps:
-            send_halo(RCV, level + 1)
-            local(RCV, level + 1)
-        wait_halo(SRC, level)
-        finish(SRC, level)
+            send_halo(RCV, level + 1, hops(level + 1))
+            local(RCV, level + 1, mine)
+        if level == 1:
+            for kind in range(2):
+                each_side(1, lambda side: side_copy(kind, 1 - side).wait_recv())
+        if wide(level):
+            around(RCV, level)
+        wait_halo(SRC, level, hops(level))
+        finish(SRC, level, mine)
+        if wide(level):
+            around(SRC, level)
 
     for back, level in enumerate((steps, steps - 1)):
         for x in range(slab_x):
             for y in range(slab_y):
                 at = (back * slab_x + x) * slab_y + y
                 leaving[pl.ds(at, devices, stride=back_rows), :] = levels[
-                    level, SRC, REACH + y, pl.ds(EDGE + x, devices, stride=slab_x), :
+                    level, SRC, pad + y, pl.ds(EDGE + x, devices, stride=slab_x), :
                 ]
 
     def back_copy(peer):
@@ -308,12 +358,12 @@
     own_back = pl.ds(pl.multiple_of(me * back_rows, 8), back_rows)
     returned[own_back, :] = leaving[own_back, :]
     for y in range(slab_y):
-        rcv_next[y] = levels[steps, RCV, REACH + y, inside, :]
-        rcv_prior[y] = levels[steps - 1, RCV, REACH + y, inside, :]
+        rcv_next[y] = levels[steps, RCV, pad + y, inside, :]
+        rcv_prior[y] = levels[steps - 1, RCV, pad + y, inside, :]
         for field in (SRC, RCV):
             for snap in range(padded.shape[0]):
                 padded[snap, field, y, half : half + cells_x, :] = levels[
-                    2 * snap + 2, field, REACH + y, inside, :
+                    2 * snap + 2, field, pad + y, inside, :
                 ]
     for plane in range(lags):
         slot = lag_order[plane]
@@ -329,9 +379,10 @@
     sent = staged.at[pl.ds(0, (devices - 1) * block)]
     pltpu.make_async_copy(sent, sent, out_send).wait()
     for level in range(steps):
-        wait_sent(RCV, level)
-        if level > 0:
-            wait_sent(SRC, level)
+        wait_sent(RCV, level, hops(level) if level > 0 else (1,))
+        wait_sent(SRC, level, hops(level))
+    for kind in range(2):
+        each_side(1, lambda side: side_copy(kind, side).wait_send())
 
     came = returned.at[pl.ds(0, (devices - 1) * back_rows)]
     pltpu.make_async_copy(came, came, back_recv).wait()
@@ -371,6 +422,7 @@
         steps = wavelet.shape[0]
         lags = lag_order.shape[0]
         half = (lags - 1) // 2
+        assert slab_y == REACH and devices > 3
         span = slab_y + 2 * REACH
         rows = -(-(span + slab_y) // 8) * 8
         f32 = jnp.float32
@@ -389,7 +441,7 @@
             like(src_now),
             like(src_old),
             like(rcv_old),
-            like(medium),
+            pltpu.VMEM((3, span, cells_x, cells_z), f32),
             scalars(wavelet),
             scalars(shot),
             like(traces),
@@ -398,10 +450,10 @@
             pltpu.VMEM((taken, 2, slab_y, cells_x + 2 * half, cells_z), f32),
             pltpu.VMEM((cells_x * rows, cells_z), f32),
             pltpu.VMEM((cells_x * rows, cells_z), f32),
-            pltpu.VMEM((steps + 1, 2, span, cells_x + 2 * EDGE, cells_z), f32),
-            pltpu.VMEM((2, slab_y, cells_x, cells_z), f32),
-            pltpu.VMEM((steps, slab_y, cells_x, cells_z), f32),
-            pltpu.VMEM((slab_y, cells_x, cells_z), f32),
+            pltpu.VMEM((steps + 1, 2, span + 2 * REACH, cells_x + 2 * EDGE, cells_z), f32),
+            pltpu.VMEM((2, span, cells_x, cells_z), f32),
+            pltpu.VMEM((steps, span, cells_x, cells_z), f32),
+            pltpu.VMEM((span, cells_x, cells_z), f32),
             pltpu.VMEM((devices * 2 * slab_x * slab_y, cells_z), f32),
             pltpu.VMEM((devices * 2 * slab_x * slab_y, cells_z), f32),
         ]
@@ -414,9 +466,11 @@
             scratch_shapes=scratch
             + [pltpu.SemaphoreType.DMA] * 4
             + [
-                pltpu.SemaphoreType.DMA((2, steps, 2)),
-                pltpu.SemaphoreType.DMA((2, steps, 2)),
+                pltpu.SemaphoreType.DMA((2, steps, 2, 2)),
+                pltpu.SemaphoreType.DMA((2, steps, 2, 2)),
                 pltpu.SemaphoreType.DMA((10,)),
+                pltpu.SemaphoreType.DMA((2, 2)),
+                pltpu.SemaphoreType.DMA((2, 2)),
             ],
             compiler_params=pltpu.CompilerParams(
                 collective_id=0, has_side_effects=True, vmem_limit_bytes=held + (4 << 20)

time: 25.5 us -> 26.1 us (1.024)
  Pallas kernels: 24.7 us -> 25.3 us
    pallas_call x1, Pallas kernels: 23.6 us -> 24.2 us  [on_device(): pl.pallas_call(functools.partial(window_kernel, devices), out_shape=shape...]
where the time goes in v3:
time: 26.1 us; the launch traced here: 25.9 us
  Pallas kernels  25.3 us (97%)
  between operations  0.64 us (2%)
    pallas_call x1, Pallas kernels, on_device(): pl.pallas_call(functools.partial(window_kernel, devices), out_shape=shape...  24.2 us
    pallas_call x1, Pallas kernels, on_device(): pl.pallas_call(deliver_kernel, out_shape=shapes, in_specs=[vmem] * 5, out...  1.07 us

profile of v3, /device:TPU:0, one launch (start us, length us, event | category | flops | bytes accessed | tf_op | source)
XLA Modules:
  0.0 25.9 jit_solution(11155146808622690735)
XLA Ops:
  0.6 24.2 %window.1 = (f32[2,32,128]{2,1,0:T(8,128)S(1)}, f32[2,32,128]{2,1,0:T(8,128)S(1)}, f32[2,32,128]{2,1,0:T(8,128)S(1)}, f32[2,32,128]{2,1,0:T(8,128)S(1)}, f32[33,2,32,128]{3,2,1,0:T(8,128)S(1)}) custom-call(f32[2,32,128]{2,1,0:T(8,128)} %src_now_in.1, f32[2,32,128]{2,1,0:T(8,128)} %src_old_in.1, f32[2,32,128]{2,1,0:T(8,128)} %bitcast.8, ...), custom_call_target="tpu_custom_call" | custom-call | tf_op jit(solution)/shard_map/window/pallas_call | solution.py:461
  24.8 1.1 %deliver.1 = (f32[2,32,128]{2,1,0:T(8,128)}, f32[2,32,128]{2,1,0:T(8,128)}, f32[2,32,128]{2,1,0:T(8,128)}, f32[2,32,128]{2,1,0:T(8,128)}, f32[33,2,32,128]{3,2,1,0:T(8,128)}) custom-call(f32[2,32,128]{2,1,0:T(8,128)S(1)} %get-tuple-element.15.refs_0_, f32[2,32,128]{2,1,0:T(8,128)S(1)} %get-tuple-element.16.refs_1_, ...), custom_call_target="tpu_custom_call" | custom-call | tf_op jit(solution)/shard_map/deliver/pallas_call | solution.py:496

commit v4 on v2

--- a/solution.py
+++ b/solution.py
@@ -12,6 +12,7 @@
 EDGE = 8
 OUTER, INNER, CENTRE = -1.0 / 12.0, 4.0 / 3.0, -2.5
 SRC, RCV = 0, 1
+PARTS = 6
 
 
 def second(window):
@@ -348,8 +349,16 @@
 
 def deliver_kernel(*refs):
     count = (len(refs) - 1) // 2
+    planes = refs[count - 1].shape[0]
+    cuts = [planes * part // PARTS for part in range(PARTS + 1)]
+    pieces = [
+        (refs[count - 1].at[pl.ds(low, high - low)], refs[2 * count - 1].at[pl.ds(low, high - low)])
+        for low, high in zip(cuts, cuts[1:])
+    ]
+    pieces += [(refs[i], refs[count + i]) for i in range(count - 1)]
     copies = [
-        pltpu.make_async_copy(refs[i], refs[count + i], refs[-1].at[i]) for i in range(count)
+        pltpu.make_async_copy(source, target, refs[-1].at[i])
+        for i, (source, target) in enumerate(pieces)
     ]
     for copy in copies:
         copy.start()
@@ -444,7 +453,7 @@
             out_shape=shapes,
             in_specs=[vmem] * 5,
             out_specs=(hbm,) * 5,
-            scratch_shapes=[pltpu.SemaphoreType.DMA((5,))],
+            scratch_shapes=[pltpu.SemaphoreType.DMA((4 + PARTS,))],
             compiler_params=pltpu.CompilerParams(vmem_limit_bytes=held + (4 << 20)),
             name="deliver",
         )(*results)

time: 25.5 us -> 25.5 us (level)
  no operation moved by 1% of the time
where the time goes in v4:
time: 25.5 us; the launch traced here: 25.4 us
  Pallas kernels  24.7 us (97%)
  between operations  0.64 us (3%)
    pallas_call x1, Pallas kernels, on_device(): pl.pallas_call(functools.partial(window_kernel, devices), out_shape=shape...  23.6 us
    pallas_call x1, Pallas kernels, on_device(): pl.pallas_call(deliver_kernel, out_shape=shapes, in_specs=[vmem] * 5, out...  1.09 us

profile of v4, /device:TPU:0, one launch (start us, length us, event | category | flops | bytes accessed | tf_op | source)
XLA Modules:
  0.0 25.4 jit_solution(5582433835014530743)
XLA Ops:
  0.6 23.6 %window.1 = (f32[2,32,128]{2,1,0:T(8,128)S(1)}, f32[2,32,128]{2,1,0:T(8,128)S(1)}, f32[2,32,128]{2,1,0:T(8,128)S(1)}, f32[2,32,128]{2,1,0:T(8,128)S(1)}, f32[33,2,32,128]{3,2,1,0:T(8,128)S(1)}) custom-call(f32[2,32,128]{2,1,0:T(8,128)} %src_now_in.1, f32[2,32,128]{2,1,0:T(8,128)} %src_old_in.1, f32[2,32,128]{2,1,0:T(8,128)} %bitcast.8, ...), custom_call_target="tpu_custom_call" | custom-call | tf_op jit(solution)/shard_map/window/pallas_call | solution.py:418
  24.3 1.1 %deliver.1 = (f32[2,32,128]{2,1,0:T(8,128)}, f32[2,32,128]{2,1,0:T(8,128)}, f32[2,32,128]{2,1,0:T(8,128)}, f32[2,32,128]{2,1,0:T(8,128)}, f32[33,2,32,128]{3,2,1,0:T(8,128)}) custom-call(f32[2,32,128]{2,1,0:T(8,128)S(1)} %get-tuple-element.15.refs_0_, f32[2,32,128]{2,1,0:T(8,128)S(1)} %get-tuple-element.16.refs_1_, ...), custom_call_target="tpu_custom_call" | custom-call | tf_op jit(solution)/shard_map/deliver/pallas_call | solution.py:451
